TPU v7x, 128 devices: a whole 4x4x4 slice. The times are simulated.
128 devices in a mesh: row: 8 (over x, core), col: 16 (over y, z).
Axes of the slice: x: 4, y: 4, z: 4, core: 2. Of those that a mesh axis runs over, the one named last changes fastest.
Arguments:
- left_factor: bfloat16 [4, 2048, 24, 4096], P(None, 'row', None, 'col'), may hold values from -0.01953125 to 0.01953125
- prev_solution: bfloat16 [24, 4096, 512], P('row', 'col'), may hold values from -6 to 6
- cross: bfloat16 [4, 2048, 512], P(None, 'row'), may hold values from -6 to 6
- inverses: bfloat16 [2, 2, 2048, 1, 4096], P(None, None, 'row', None, 'col'), as said below
- coupling: bfloat16 [2, 2048, 1, 4096], P(None, 'row', None, 'col'), may hold values from -0.09375 to 0.09375
- prior_cov: float32 [512, 512], P('col'), may hold values from -6 to 6
Outputs:
- solved: bfloat16 [4, 2048, 512], P(None, 'row')
- pred_cov: float32 [512, 512], P('col')
Inputs may be any that keep to these rules, and one draw needn't show every extreme that they name: Each block of inverses is lower triangular in natural order, with diagonal entries from 0.5 to 1.5.
All inputs are finite; a program needn't handle non-finite values.
Results may differ from a plain program's by a relative error of at most 0.0056.
Values may be sent and summed in bfloat16 or wider, within the bound.
No kernel may reach another device: no remote copies, remote signals or barrier semaphores. Data moves between devices by JAX's collectives and lax.ppermute only.
A program may use at most 64 MiB of HBM per device.

v0:
```python
import jax
import jax.numpy as jnp
from jax import lax
from jax.sharding import PartitionSpec as P

S = 8192


def from_root(shard, axis, root):
    return lax.dynamic_index_in_dim(lax.all_gather(shard, axis), root, 0, keepdims=False)


def filled_up(lines, peers):
    spare = -len(lines) % peers
    return jnp.pad(lines, [(0, spare)] + [(0, 0)] * (lines.ndim - 1))


def in_order(blocks, dim):
    shape = list(blocks.shape[1:])
    shape[dim] *= blocks.shape[0]
    return jnp.moveaxis(blocks, 0, dim).reshape(shape)


def from_everyone(shard, axis):
    peers = lax.axis_size(axis)
    return lax.all_to_all(
        jnp.broadcast_to(shard[None], (peers, *shard.shape)), axis, 0, 0, tiled=True
    )


def gather_directly(shard, axis, dim):
    return in_order(from_everyone(shard, axis), dim)


def cut_along(shard, dim, peers):
    shape = shard.shape
    blocks = shard.reshape(*shape[:dim], peers, shape[dim] // peers, *shape[dim + 1 :])
    return jnp.moveaxis(blocks, dim, 0)


def sent_and_summed(shard, axis, dim):
    blocks = cut_along(shard, dim, lax.axis_size(axis))
    arrived = lax.all_to_all(blocks, axis, split_axis=0, concat_axis=0, tiled=True)
    return arrived.sum(axis=0)


def sum_by_parts(shard, axes):
    lines = shard.reshape(-1, shard.shape[-1])
    padded = filled_up(lines, lax.axis_size(axes))
    whole = gather_directly(sent_and_summed(padded, axes, 0), axes, 0)
    return lax.slice_in_dim(whole, 0, len(lines)).reshape(shard.shape)


def over_copies(shard, axis):
    return from_everyone(shard, axis).astype(jnp.float32).sum(axis=0)


def apply_block(matrix, values):
    return jnp.einsum("atbu,bum->atm", matrix, values, preferred_element_type=jnp.float32)


def spread_rows(values):
    n_row = lax.axis_size("row")
    n_col = lax.axis_size("col")
    col_id = lax.axis_index("col")
    rounds, tile, sites = values.shape
    group = n_col // n_row
    grouped = values.reshape(rounds // group, group, tile, sites)
    picked = lax.dynamic_index_in_dim(grouped, col_id // n_row, 1, keepdims=False)
    return from_root(picked, "row", col_id % n_row)


def column_sum(values):
    return sum_by_parts(values, "col")


def solve_rounded(values):
    return sum_by_parts(values, "col").astype(jnp.bfloat16)


def outer_rows(solution):
    share = solution.shape[2] // lax.axis_size("col")
    own = lax.dynamic_slice_in_dim(solution, lax.axis_index("col") * share, share, 2)
    return jnp.einsum("atm,atn->mn", own, solution, preferred_element_type=jnp.float32)


def body(left_factor, prev_solution, cross, inverses, coupling, prior_cov):
    half = coupling.shape[0]
    pre = jnp.einsum(
        "atbu,bum->atm",
        left_factor,
        lax.all_gather(prev_solution, "row", axis=0, tiled=True),
        preferred_element_type=jnp.float32,
    )
    cross_first = cross[:half].astype(jnp.float32)
    cross_second = cross[half:].astype(jnp.float32)
    pre_first = sum_by_parts(pre[:half], "col")
    first_rhs = (cross_first - pre_first).astype(jnp.bfloat16)
    solved_first = solve_rounded(apply_block(inverses[0], spread_rows(first_rhs)))
    linked = column_sum(pre[half:] + apply_block(coupling, spread_rows(solved_first)))
    second_rhs = (cross_second - linked).astype(jnp.bfloat16)
    solved_second = solve_rounded(apply_block(inverses[1], spread_rows(second_rhs)))
    solved_all = jnp.concatenate([solved_first, solved_second], axis=0)
    outer_total = over_copies(outer_rows(solved_all).astype(jnp.bfloat16), "row").astype(
        jnp.float32
    )
    pred_cov = prior_cov - outer_total / S
    return (solved_all, pred_cov)


def solution(mesh):
    placed = (
        P(None, "row", None, "col"),
        P("row", "col", None),
        P(None, "row", None),
        P(None, None, "row", None, "col"),
        P(None, "row", None, "col"),
        P("col", None),
    )
    return jax.shard_map(
        body,
        mesh=mesh,
        in_specs=placed,
        out_specs=(P(None, "row", None), P("col", None)),
        check_vma=False,
    )
```

profile of v0, /device:TPU:1, one launch (start us, length us, event | category | flops | bytes accessed | tf_op | source)
XLA Modules:
  0.0 326.6 jit_solution(15073894378876235162)
XLA Ops:
  7.2 0.7 all-gather.8.cloned.1.call-update
  7.9 46.3 %all-gather.8.cloned.1.call-done = bf16[24,256,512]{2,1,0:T(8,128)(2,1)} async-done(((bf16[3,256,512]{2,1,0:T(8,128)(2,1)}), bf16[24,256,512]{2,1,0:T(8,128)(2,1)}) %all-gather.8.cloned.1.call-update) | async-done | bytes 6291472 | tf_op jit(solution)/shard_map/all_gather | solution.py:92
  54.2 14.2 %fusion.3 = f32[4,256,512]{2,1,0:T(8,128)S(1)} fusion(bf16[24,256,512]{2,1,0:T(8,128)(2,1)} %all-gather.8.cloned.1.call-done, bf16[4,256,24,256]{3,2,1,0:T(8,128)(2,1)} %param.6), kind=kOutput, calls=%fused_computation.3 | convolution fusion | flops 6442450944 | bytes 20971520 | tf_op jit(solution)/shard_map/atbu,bum->atm/dot_general | solution.py:89
  68.5 22.4 %all_to_all.45 = f32[16,32,512]{2,1,0:T(8,128)S(1)} all-to-all(f32[16,32,512]{2,1,0:T(8,128)S(1)} %bitcast.52), channel_id=1, replica_groups=mesh['row'=8,'col'=16] {'col'}, dimensions={0} | all-to-all | bytes 2097152 | tf_op jit(solution)/shard_map/all_to_all | solution.py:43
  91.0 1.1 broadcast_in_dim.10
  92.1 3.9 %all-to-all-start.1 = ((f32[16,32,512]{2,1,0:T(8,128)}), f32[16,32,512]{2,1,0:T(8,128)S(1)}, u32[]{:S(2)}, u32[]{:S(2)}) async-start(f32[16,32,512]{2,1,0:T(8,128)} %broadcast_in_dim.10), calls=%async_computation.1 | async-start | bytes 2097152 | tf_op jit(solution)/shard_map/all_to_all | solution.py:26
  96.1 2.3 fusion.26
  98.4 12.7 %all-to-all-done.1 = f32[16,32,512]{2,1,0:T(8,128)S(1)} async-done(((f32[16,32,512]{2,1,0:T(8,128)}), f32[16,32,512]{2,1,0:T(8,128)S(1)}, u32[]{:S(2)}, u32[]{:S(2)}) %all-to-all-start.1) | async-done | bytes 1048608 | tf_op jit(solution)/shard_map/all_to_all | solution.py:26
  111.0 1.7 fusion.11
  112.9 1.8 fusion.27
  114.6 22.8 %all-gather.10.cloned.1.call-done = bf16[8,256,512]{2,1,0:T(8,128)(2,1)} async-done(((bf16[1,256,512]{2,1,0:T(8,128)(2,1)}), bf16[8,256,512]{2,1,0:T(8,128)(2,1)}) %all-gather.10.cloned.1.call-update) | async-done | bytes 2097168 | tf_op jit(solution)/shard_map/all_gather | solution.py:10
  137.5 1.2 convolution_bitcast_fusion.2
  138.7 22.4 %all_to_all.46 = f32[16,32,512]{2,1,0:T(8,128)S(1)} all-to-all(f32[16,32,512]{2,1,0:T(8,128)S(1)} %convolution_bitcast_fusion.2), channel_id=1, replica_groups=mesh['row'=8,'col'=16] {'col'}, dimensions={0} | all-to-all | bytes 2097152 | tf_op jit(solution)/shard_map/all_to_all | solution.py:43
  161.1 0.1 reduce_sum.46
  161.3 12.8 %all_to_all.47 = bf16[16,32,512]{2,1,0:T(8,128)(2,1)S(1)} all-to-all(bf16[16,32,512]{2,1,0:T(8,128)(2,1)S(1)} %broadcast_in_dim.11), channel_id=1, replica_groups=mesh['row'=8,'col'=16] {'col'}, dimensions={0} | all-to-all | bytes 1048576 | tf_op jit(solution)/shard_map/all_to_all | solution.py:26
  174.0 0.7 constant_dynamic-slice_fusion
  174.8 25.1 %all-gather.12.cloned.1.call-done = bf16[8,256,512]{2,1,0:T(8,128)(2,1)} async-done(((bf16[1,256,512]{2,1,0:T(8,128)(2,1)}), bf16[8,256,512]{2,1,0:T(8,128)(2,1)}) %all-gather.12.cloned.1.call-update) | async-done | bytes 2097168 | tf_op jit(solution)/shard_map/all_gather | solution.py:10
  199.9 1.2 fusion.8
  201.2 22.4 %all_to_all.48 = f32[16,32,512]{2,1,0:T(8,128)S(1)} all-to-all(f32[16,32,512]{2,1,0:T(8,128)S(1)} %bitcast.51), channel_id=1, replica_groups=mesh['row'=8,'col'=16] {'col'}, dimensions={0} | all-to-all | bytes 2097152 | tf_op jit(solution)/shard_map/all_to_all | solution.py:43
  223.7 0.1 broadcast_in_dim.12
  223.8 18.5 %all_to_all.49 = f32[16,32,512]{2,1,0:T(8,128)S(1)} all-to-all(f32[16,32,512]{2,1,0:T(8,128)S(1)} %broadcast_in_dim.12), channel_id=1, replica_groups=mesh['row'=8,'col'=16] {'col'}, dimensions={0} | all-to-all | bytes 2097152 | tf_op jit(solution)/shard_map/all_to_all | solution.py:26
  242.3 0.8 fusion.10
  243.1 25.2 %all-gather.14.cloned.1.call-done = bf16[8,256,512]{2,1,0:T(8,128)(2,1)} async-done(((bf16[1,256,512]{2,1,0:T(8,128)(2,1)}), bf16[8,256,512]{2,1,0:T(8,128)(2,1)}) %all-gather.14.cloned.1.call-update) | async-done | bytes 2097168 | tf_op jit(solution)/shard_map/all_gather | solution.py:10
  268.3 1.2 convolution_bitcast_fusion
  269.6 22.4 %all_to_all.50 = f32[16,32,512]{2,1,0:T(8,128)S(1)} all-to-all(f32[16,32,512]{2,1,0:T(8,128)S(1)} %convolution_bitcast_fusion), channel_id=1, replica_groups=mesh['row'=8,'col'=16] {'col'}, dimensions={0} | all-to-all | bytes 2097152 | tf_op jit(solution)/shard_map/all_to_all | solution.py:43
  292.1 0.8 broadcast_in_dim.13
  292.9 3.9 %all-to-all-start.7 = ((bf16[16,32,512]{2,1,0:T(8,128)(2,1)}), bf16[16,32,512]{2,1,0:T(8,128)(2,1)S(1)}, u32[]{:S(2)}, u32[]{:S(2)}) async-start(bf16[16,32,512]{2,1,0:T(8,128)(2,1)} %broadcast_in_dim.13), calls=%async_computation.7 | async-start | bytes 1048576 | tf_op jit(solution)/shard_map/all_to_all | solution.py:26
  296.8 9.1 %all-to-all-done.7 = bf16[16,32,512]{2,1,0:T(8,128)(2,1)S(1)} async-done(((bf16[16,32,512]{2,1,0:T(8,128)(2,1)}), bf16[16,32,512]{2,1,0:T(8,128)(2,1)S(1)}, u32[]{:S(2)}, u32[]{:S(2)}) %all-to-all-start.7) | async-done | bytes 524320 | tf_op jit(solution)/shard_map/all_to_all | solution.py:26
  306.0 0.1 pad_maximum_fusion
  306.1 0.4 fusion.9
  306.6 12.9 %all_to_all.51 = bf16[8,32,512]{2,1,0:T(8,128)(2,1)S(1)} all-to-all(bf16[8,32,512]{2,1,0:T(8,128)(2,1)S(1)} %broadcast_in_dim.14), channel_id=1, replica_groups=mesh['row'=8,'col'=16] {'row'}, dimensions={0} | all-to-all | bytes 524288 | tf_op jit(solution)/shard_map/all_to_all | solution.py:26
  319.5 0.6 multiply_subtract_fusion
  (24 shorter events, 0.6 us)
Async XLA Ops:
  7.2 192.8 %copy-start = (bf16[2,256,1,256]{3,1,2,0:T(8,128)(2,1)S(1)}, bf16[2,256,1,256]{3,1,2,0:T(8,128)(2,1)}, u32[]{:S(2)}) copy-start(bf16[2,256,1,256]{3,1,2,0:T(8,128)(2,1)} %param.10) | copy-start | bytes 786436
  7.2 47.1 %all-gather.8.cloned.1.call-start = ((), (), s32[]{:S(2)}) async-start(), calls=%async_computation.9 | async-start | bytes 7077888 | tf_op jit(solution)/shard_map/all_gather | solution.py:92
  92.1 19.0 %all-to-all-start.1 = ((f32[16,32,512]{2,1,0:T(8,128)}), f32[16,32,512]{2,1,0:T(8,128)S(1)}, u32[]{:S(2)}, u32[]{:S(2)}) async-start(f32[16,32,512]{2,1,0:T(8,128)} %broadcast_in_dim.10), calls=%async_computation.1 | async-start | bytes 2097152 | tf_op jit(solution)/shard_map/all_to_all | solution.py:26
  96.0 41.4 %all-gather.10.cloned.1.call-start = ((), (), s32[]{:S(2)}) async-start(), calls=%async_computation.10 | async-start | bytes 2359296 | tf_op jit(solution)/shard_map/all_gather | solution.py:10
  112.8 87.1 %all-gather.12.cloned.1.call-start = ((), (), s32[]{:S(2)}) async-start(), calls=%async_computation.11 | async-start | bytes 2359296 | tf_op jit(solution)/shard_map/all_gather | solution.py:10
  174.8 93.5 %all-gather.14.cloned.1.call-start = ((), (), s32[]{:S(2)}) async-start(), calls=%async_computation.12 | async-start | bytes 2359296 | tf_op jit(solution)/shard_map/all_gather | solution.py:10
  223.6 18.7 %copy-start.2 = (bf16[2,256,512]{2,1,0:T(8,128)(2,1)S(1)}, bf16[2,256,512]{2,1,0:T(8,128)(2,1)}, u32[]{:S(2)}) copy-start(bf16[2,256,512]{2,1,0:T(8,128)(2,1)} %get-tuple-element.2) | copy-start | bytes 1572868
  223.7 44.6 %copy-start.3 = (bf16[1,2,256,1,256]{4,2,3,1,0:T(8,128)(2,1)S(1)}, bf16[1,2,256,1,256]{4,2,3,1,0:T(8,128)(2,1)}, u32[]{:S(2)}) copy-start(bf16[1,2,256,1,256]{4,2,3,1,0:T(8,128)(2,1)} %get-tuple-element.5) | copy-start | bytes 786436
  292.9 13.1 %all-to-all-start.7 = ((bf16[16,32,512]{2,1,0:T(8,128)(2,1)}), bf16[16,32,512]{2,1,0:T(8,128)(2,1)S(1)}, u32[]{:S(2)}, u32[]{:S(2)}) async-start(bf16[16,32,512]{2,1,0:T(8,128)(2,1)} %broadcast_in_dim.13), calls=%async_computation.7 | async-start | bytes 1048576 | tf_op jit(solution)/shard_map/all_to_all | solution.py:26
  306.1 14.0 %copy-start.1 = (bf16[4,256,512]{2,1,0:T(8,128)(2,1)}, bf16[4,256,512]{2,1,0:T(8,128)(2,1)S(1)}, u32[]{:S(2)}) copy-start(bf16[4,256,512]{2,1,0:T(8,128)(2,1)S(1)} %pad_maximum_fusion) | copy-start | bytes 3145732
  306.1 13.4 %copy-start.4 = (f32[32,512]{1,0:T(8,128)S(1)}, f32[32,512]{1,0:T(8,128)}, u32[]{:S(2)}) copy-start(f32[32,512]{1,0:T(8,128)} %param.11) | copy-start | bytes 196612
Sparse Core Ops, SparseCore 0:
  9.7 44.4 all-gather.7
  112.9 24.4 all-gather.9
  174.9 25.0 all-gather.11
  243.2 25.0 all-gather.13
where the time goes:
time: 327 us
  waiting for transfers between devices  142 us (43%)
  blocking collectives  134 us (41%)
  matrix products  18.3 us (6%)
  between operations  13.9 us (4%)
  starting transfers between devices  8 us (2%)
  local copies, waits for them, and re-layouts  7.02 us (2%)
  other arithmetic  3.55 us (1%)
    all_to_all x4, blocking collectives, sent_and_summed(): lax.all_to_all(blocks, axis, split_axis=0, concat_axis=0, tiled=True)  89.7 us
    all_gather x3, waiting for transfers between devices, from_root(): lax.all_gather(shard, axis)  73.1 us
    all_gather x1, waiting for transfers between devices, body(): lax.all_gather(prev_solution, 'row', axis=0, tiled=True)  46.3 us
    all_to_all x3, blocking collectives, from_everyone(): lax.all_to_all(jnp.broadcast_to(shard[None], (peers, *shard.shape)), axis...  44.1 us
    all_to_all x2, waiting for transfers between devices, from_everyone(): lax.all_to_all(jnp.broadcast_to(shard[None], (peers, *shard.shape)), axis...  21.8 us
    dot_general x1, matrix products, body(): jnp.einsum('atbu,bum->atm', left_factor, lax.all_gather(prev_solution, 'r...  14.2 us
    all_to_all x2, starting transfers between devices, from_everyone(): lax.all_to_all(jnp.broadcast_to(shard[None], (peers, *shard.shape)), axis...  7.83 us
  transfers between devices with their start and end apart: 6, of which 6 were waited for; matrix products, arithmetic and copies ran while one was open for 1% of the time, Pallas kernels for 0%

commit v1 on v0

--- a/solution.py
+++ b/solution.py
@@ -4,6 +4,11 @@
 from jax.sharding import PartitionSpec as P
 
 S = 8192
+
+
+def gather_over(block, mesh_axis, dim):
+    repeated = jnp.stack([block] * lax.axis_size(mesh_axis))
+    return jnp.concatenate(lax.all_to_all(repeated, mesh_axis, 0, 0), axis=dim)
 
 
 def from_root(shard, axis, root):
@@ -89,7 +94,7 @@
     pre = jnp.einsum(
         "atbu,bum->atm",
         left_factor,
-        lax.all_gather(prev_solution, "row", axis=0, tiled=True),
+        gather_over(prev_solution, "row", 0),
         preferred_element_type=jnp.float32,
     )
     cross_first = cross[:half].astype(jnp.float32)

time: 327 us -> 358 us (1.095)
  blocking collectives: 134 us -> 211 us
  waiting for transfers between devices: 142 us -> 94.7 us
    all_to_all x0 -> x1, blocking collectives: none -> 77.7 us  [gather_over(): return jnp.concatenate(lax.all_to_all(repeated, mesh_axis, 0, 0), axis=dim)]
    all_gather x1 -> x0, waiting for transfers between devices: 46.3 us -> none  [body(): lax.all_gather(prev_solution, 'row', axis=0, tiled=True)]
  transfers between devices with their start and end apart: 6 -> 5, of which waited for: 6 -> 5; matrix products, arithmetic and copies ran while one was open for 1% -> 1% of each run, Pallas kernels for 0% -> 0%
where the time goes in v1:
time: 358 us; the launch traced here: 357 us
  blocking collectives  211 us (59%)
  waiting for transfers between devices  94.7 us (26%)
  matrix products  16.3 us (5%)
  between operations  13.9 us (4%)
  local copies, waits for them, and re-layouts  8.83 us (2%)
  starting transfers between devices  8.43 us (2%)
    all_to_all x4, blocking collectives, sent_and_summed(): lax.all_to_all(blocks, axis, split_axis=0, concat_axis=0, tiled=True)  89.5 us
    all_to_all x1, blocking collectives, gather_over(): return jnp.concatenate(lax.all_to_all(repeated, mesh_axis, 0, 0), axis=dim)  77.7 us
    all_gather x3, waiting for transfers between devices, from_root(): lax.all_gather(shard, axis)  73.3 us
    all_to_all x3, blocking collectives, from_everyone(): lax.all_to_all(jnp.broadcast_to(shard[None], (peers, *shard.shape)), axis...  44 us
    all_to_all x2, waiting for transfers between devices, from_everyone(): lax.all_to_all(jnp.broadcast_to(shard[None], (peers, *shard.shape)), axis...  21.4 us
    dot_general x1, matrix products, body(): jnp.einsum('atbu,bum->atm', left_factor, gather_over(prev_solution, 'row'...  12.2 us
    all_to_all x2, starting transfers between devices, from_everyone(): lax.all_to_all(jnp.broadcast_to(shard[None], (peers, *shard.shape)), axis...  8.31 us
  transfers between devices with their start and end apart: 5, of which 5 were waited for; matrix products, arithmetic and copies ran while one was open for 1% of the time, Pallas kernels for 0%

profile of v1, /device:TPU:1, one launch (start us, length us, event | category | flops | bytes accessed | tf_op | source)
XLA Modules:
  0.0 357.1 jit_solution(7146535219173262916)
XLA Ops:
  7.2 1.8 stack.2
  9.0 77.7 %all_to_all.50 = bf16[8,3,256,512]{3,2,1,0:T(8,128)(2,1)S(1)} all-to-all(bf16[8,3,256,512]{3,2,1,0:T(8,128)(2,1)S(1)} %stack.2), channel_id=1, replica_groups=mesh['row'=8,'col'=16] {'row'}, dimensions={0} | all-to-all | bytes 12582912 | tf_op jit(solution)/shard_map/all_to_all | solution.py:11
  86.8 12.2 %fusion.2 = f32[4,256,512]{2,1,0:T(8,128)S(1)} fusion(bf16[24,256,512,1]{2,1,0,3:T(8,128)(2,1)S(1)} %bitcast.48, bf16[4,256,24,256]{3,2,1,0:T(8,128)(2,1)} %param.6), kind=kOutput, calls=%fused_computation.2 | convolution fusion | flops 6442450944 | bytes 20971520 | tf_op jit(solution)/shard_map/atbu,bum->atm/dot_general | solution.py:94
  99.0 22.2 %all_to_all.51 = f32[16,32,512]{2,1,0:T(8,128)S(1)} all-to-all(f32[16,32,512]{2,1,0:T(8,128)S(1)} %bitcast.52), channel_id=1, replica_groups=mesh['row'=8,'col'=16] {'col'}, dimensions={0} | all-to-all | bytes 2097152 | tf_op jit(solution)/shard_map/all_to_all | solution.py:48
  121.3 1.1 broadcast_in_dim.10
  122.4 4.4 %all-to-all-start.2 = ((f32[16,32,512]{2,1,0:T(8,128)}), f32[16,32,512]{2,1,0:T(8,128)S(1)}, u32[]{:S(2)}, u32[]{:S(2)}) async-start(f32[16,32,512]{2,1,0:T(8,128)} %broadcast_in_dim.10), calls=%async_computation.2 | async-start | bytes 2097152 | tf_op jit(solution)/shard_map/all_to_all | solution.py:31
  126.8 2.3 fusion.23
  129.1 12.2 %all-to-all-done.2 = f32[16,32,512]{2,1,0:T(8,128)S(1)} async-done(((f32[16,32,512]{2,1,0:T(8,128)}), f32[16,32,512]{2,1,0:T(8,128)S(1)}, u32[]{:S(2)}, u32[]{:S(2)}) %all-to-all-start.2) | async-done | bytes 1048608 | tf_op jit(solution)/shard_map/all_to_all | solution.py:31
  141.3 1.7 fusion.8
  143.1 1.8 fusion.24
  144.9 23.0 %all-gather.7.cloned.1.call-done = bf16[8,256,512]{2,1,0:T(8,128)(2,1)} async-done(((bf16[1,256,512]{2,1,0:T(8,128)(2,1)}), bf16[8,256,512]{2,1,0:T(8,128)(2,1)}) %all-gather.7.cloned.1.call-update) | async-done | bytes 2097168 | tf_op jit(solution)/shard_map/all_gather | solution.py:15
  167.9 1.2 convolution_bitcast_fusion.2
  169.1 22.4 %all_to_all.52 = f32[16,32,512]{2,1,0:T(8,128)S(1)} all-to-all(f32[16,32,512]{2,1,0:T(8,128)S(1)} %convolution_bitcast_fusion.2), channel_id=1, replica_groups=mesh['row'=8,'col'=16] {'col'}, dimensions={0} | all-to-all | bytes 2097152 | tf_op jit(solution)/shard_map/all_to_all | solution.py:48
  191.6 0.1 reduce_sum.46
  191.7 12.7 %all_to_all.53 = bf16[16,32,512]{2,1,0:T(8,128)(2,1)S(1)} all-to-all(bf16[16,32,512]{2,1,0:T(8,128)(2,1)S(1)} %broadcast_in_dim.11), channel_id=1, replica_groups=mesh['row'=8,'col'=16] {'col'}, dimensions={0} | all-to-all | bytes 1048576 | tf_op jit(solution)/shard_map/all_to_all | solution.py:31
  204.4 0.7 constant_dynamic-slice_fusion
  205.2 25.1 %all-gather.9.cloned.1.call-done = bf16[8,256,512]{2,1,0:T(8,128)(2,1)} async-done(((bf16[1,256,512]{2,1,0:T(8,128)(2,1)}), bf16[8,256,512]{2,1,0:T(8,128)(2,1)}) %all-gather.9.cloned.1.call-update) | async-done | bytes 2097168 | tf_op jit(solution)/shard_map/all_gather | solution.py:15
  230.4 1.2 fusion.5
  231.6 22.4 %all_to_all.54 = f32[16,32,512]{2,1,0:T(8,128)S(1)} all-to-all(f32[16,32,512]{2,1,0:T(8,128)S(1)} %bitcast.51), channel_id=1, replica_groups=mesh['row'=8,'col'=16] {'col'}, dimensions={0} | all-to-all | bytes 2097152 | tf_op jit(solution)/shard_map/all_to_all | solution.py:48
  254.1 0.1 broadcast_in_dim.12
  254.3 18.5 %all_to_all.55 = f32[16,32,512]{2,1,0:T(8,128)S(1)} all-to-all(f32[16,32,512]{2,1,0:T(8,128)S(1)} %broadcast_in_dim.12), channel_id=1, replica_groups=mesh['row'=8,'col'=16] {'col'}, dimensions={0} | all-to-all | bytes 2097152 | tf_op jit(solution)/shard_map/all_to_all | solution.py:31
  272.7 0.8 fusion.7
  273.5 25.2 %all-gather.11.cloned.1.call-done = bf16[8,256,512]{2,1,0:T(8,128)(2,1)} async-done(((bf16[1,256,512]{2,1,0:T(8,128)(2,1)}), bf16[8,256,512]{2,1,0:T(8,128)(2,1)}) %all-gather.11.cloned.1.call-update) | async-done | bytes 2097168 | tf_op jit(solution)/shard_map/all_gather | solution.py:15
  298.7 1.2 convolution_bitcast_fusion
  300.0 22.4 %all_to_all.56 = f32[16,32,512]{2,1,0:T(8,128)S(1)} all-to-all(f32[16,32,512]{2,1,0:T(8,128)S(1)} %convolution_bitcast_fusion), channel_id=1, replica_groups=mesh['row'=8,'col'=16] {'col'}, dimensions={0} | all-to-all | bytes 2097152 | tf_op jit(solution)/shard_map/all_to_all | solution.py:48
  322.5 0.8 broadcast_in_dim.13
  323.3 3.9 %all-to-all-start.8 = ((bf16[16,32,512]{2,1,0:T(8,128)(2,1)}), bf16[16,32,512]{2,1,0:T(8,128)(2,1)S(1)}, u32[]{:S(2)}, u32[]{:S(2)}) async-start(bf16[16,32,512]{2,1,0:T(8,128)(2,1)} %broadcast_in_dim.13), calls=%async_computation.8 | async-start | bytes 1048576 | tf_op jit(solution)/shard_map/all_to_all | solution.py:31
  327.3 9.1 %all-to-all-done.8 = bf16[16,32,512]{2,1,0:T(8,128)(2,1)S(1)} async-done(((bf16[16,32,512]{2,1,0:T(8,128)(2,1)}), bf16[16,32,512]{2,1,0:T(8,128)(2,1)S(1)}, u32[]{:S(2)}, u32[]{:S(2)}) %all-to-all-start.8) | async-done | bytes 524320 | tf_op jit(solution)/shard_map/all_to_all | solution.py:31
  336.4 0.1 pad_maximum_fusion
  336.5 0.4 fusion.6
  337.0 12.8 %all_to_all.57 = bf16[8,32,512]{2,1,0:T(8,128)(2,1)S(1)} all-to-all(bf16[8,32,512]{2,1,0:T(8,128)(2,1)S(1)} %broadcast_in_dim.14), channel_id=1, replica_groups=mesh['row'=8,'col'=16] {'row'}, dimensions={0} | all-to-all | bytes 524288 | tf_op jit(solution)/shard_map/all_to_all | solution.py:31
  349.9 0.6 multiply_subtract_fusion
  (23 shorter events, 0.6 us)
Async XLA Ops:
  7.2 223.2 %copy-start = (bf16[2,256,1,256]{3,1,2,0:T(8,128)(2,1)S(1)}, bf16[2,256,1,256]{3,1,2,0:T(8,128)(2,1)}, u32[]{:S(2)}) copy-start(bf16[2,256,1,256]{3,1,2,0:T(8,128)(2,1)} %param.10) | copy-start | bytes 786436
  122.4 19.0 %all-to-all-start.2 = ((f32[16,32,512]{2,1,0:T(8,128)}), f32[16,32,512]{2,1,0:T(8,128)S(1)}, u32[]{:S(2)}, u32[]{:S(2)}) async-start(f32[16,32,512]{2,1,0:T(8,128)} %broadcast_in_dim.10), calls=%async_computation.2 | async-start | bytes 2097152 | tf_op jit(solution)/shard_map/all_to_all | solution.py:31
  126.8 41.1 %all-gather.7.cloned.1.call-start = ((), (), s32[]{:S(2)}) async-start(), calls=%async_computation.10 | async-start | bytes 2359296 | tf_op jit(solution)/shard_map/all_gather | solution.py:15
  143.1 87.3 %all-gather.9.cloned.1.call-start = ((), (), s32[]{:S(2)}) async-start(), calls=%async_computation.11 | async-start | bytes 2359296 | tf_op jit(solution)/shard_map/all_gather | solution.py:15
  205.2 93.5 %all-gather.11.cloned.1.call-start = ((), (), s32[]{:S(2)}) async-start(), calls=%async_computation.12 | async-start | bytes 2359296 | tf_op jit(solution)/shard_map/all_gather | solution.py:15
  254.0 18.7 %copy-start.2 = (bf16[2,256,512]{2,1,0:T(8,128)(2,1)S(1)}, bf16[2,256,512]{2,1,0:T(8,128)(2,1)}, u32[]{:S(2)}) copy-start(bf16[2,256,512]{2,1,0:T(8,128)(2,1)} %get-tuple-element.2) | copy-start | bytes 1572868
  254.1 44.6 %copy-start.3 = (bf16[1,2,256,1,256]{4,2,3,1,0:T(8,128)(2,1)S(1)}, bf16[1,2,256,1,256]{4,2,3,1,0:T(8,128)(2,1)}, u32[]{:S(2)}) copy-start(bf16[1,2,256,1,256]{4,2,3,1,0:T(8,128)(2,1)} %get-tuple-element.5) | copy-start | bytes 786436
  323.3 13.1 %all-to-all-start.8 = ((bf16[16,32,512]{2,1,0:T(8,128)(2,1)}), bf16[16,32,512]{2,1,0:T(8,128)(2,1)S(1)}, u32[]{:S(2)}, u32[]{:S(2)}) async-start(bf16[16,32,512]{2,1,0:T(8,128)(2,1)} %broadcast_in_dim.13), calls=%async_computation.8 | async-start | bytes 1048576 | tf_op jit(solution)/shard_map/all_to_all | solution.py:31
  336.5 14.0 %copy-start.1 = (bf16[4,256,512]{2,1,0:T(8,128)(2,1)}, bf16[4,256,512]{2,1,0:T(8,128)(2,1)S(1)}, u32[]{:S(2)}) copy-start(bf16[4,256,512]{2,1,0:T(8,128)(2,1)S(1)} %pad_maximum_fusion) | copy-start | bytes 3145732
  336.5 13.4 %copy-start.4 = (f32[32,512]{1,0:T(8,128)S(1)}, f32[32,512]{1,0:T(8,128)}, u32[]{:S(2)}) copy-start(f32[32,512]{1,0:T(8,128)} %param.11) | copy-start | bytes 196612
Sparse Core Ops, SparseCore 0:
  143.2 24.6 all-gather.6
  205.3 25.0 all-gather.8
  273.6 25.0 all-gather.10
